TPU v7x, 256 devices: a whole 4x4x8 slice. The times are simulated.
256 devices in a mesh: mode: 16 (over x_hi, y, core), site: 16 (over z, x_lo).
Axes of the slice: x: 4 (x_hi: 2, x_lo: 2; x = x_hi * 2 + x_lo), y: 4, z: 8, core: 2. Of those that a mesh axis runs over, the one named last changes fastest.
Arguments:
- eigvecs: bfloat16 [2, 64, 3, 110592], P(None, 'mode', None, 'site'), may hold values from -6 to 6
- perams: bfloat16 [2, 16, 64, 64], replicated, may hold values from -0.75 to 0.75
- momenta: int32 [2, 3], replicated, may hold values from -2 to 2
- spins: int32 [16, 3], replicated, may hold values from 0 to 15
- pair_combs: int32 [16, 2], P('site'), may hold values from 0 to 15
- pair_moms: int32 [16, 2], P('site'), may hold values from 0 to 1
Outputs:
- exchange: float32 [16, 2, 64, 64], P('site', None, 'mode')
All inputs are finite; a program needn't handle non-finite values.
Results may differ from a plain program's by a relative error of at most 0.018.
Values may be sent and summed in bfloat16 or wider, within the bound.
No kernel may reach another device: no remote copies, remote signals or barrier semaphores. Data moves between devices by JAX's collectives and lax.ppermute only.
A program may use at most 64 MiB of HBM per device.

v0:
```python
import jax
import jax.numpy as jnp
from jax import lax
from jax.sharding import PartitionSpec as P

LAT = 48


def hartley(momenta, glob):
    coord_x = glob // (LAT * LAT)
    coord_y = glob // LAT % LAT
    coord_z = glob % LAT
    wave = (
        momenta[:, 0:1] * coord_x[None]
        + momenta[:, 1:2] * coord_y[None]
        + momenta[:, 2:3] * coord_z[None]
    ) % LAT
    theta = wave.astype(jnp.float32) * (2.0 * jnp.pi / LAT)
    return jnp.cos(theta) + jnp.sin(theta)


def body(eigvecs, perams, momenta, spins, pair_combs, pair_moms):
    nslice, mode_dev, _, site_dev = eigvecs.shape
    nmode = perams.shape[-1]
    nspin = perams.shape[1]
    ncomb = spins.shape[0]
    nmom = momenta.shape[0]
    comb_dev = ncomb // lax.axis_size("site")
    first_mode = lax.axis_index("mode") * mode_dev
    gathered = lax.all_gather(eigvecs, "mode", axis=1, tiled=True)
    glob = lax.axis_index("site") * site_dev + jnp.arange(site_dev, dtype=jnp.int32)
    phase = hartley(momenta, glob)

    def triplet_part(vectors):
        floats = vectors.astype(jnp.float32)
        own_modes = lax.dynamic_slice_in_dim(floats, first_mode, mode_dev, 0)
        left = own_modes[:, None]
        right = floats[None]
        cross_0 = left[:, :, 1] * right[:, :, 2] - left[:, :, 2] * right[:, :, 1]
        cross_1 = left[:, :, 2] * right[:, :, 0] - left[:, :, 0] * right[:, :, 2]
        cross_2 = left[:, :, 0] * right[:, :, 1] - left[:, :, 1] * right[:, :, 0]
        diquark = jnp.stack([cross_0, cross_1, cross_2], axis=2).astype(jnp.bfloat16)
        weighted = (phase[:, None, None, :] * floats[None]).astype(jnp.bfloat16)
        product = lax.dot_general(
            diquark.reshape(mode_dev * nmode, 3 * site_dev),
            weighted.reshape(nmom * nmode, 3 * site_dev),
            (((1,), (1,)), ((), ())),
            preferred_element_type=jnp.float32,
        )
        return product.reshape(mode_dev, nmode, nmom, nmode)

    partial_sums = lax.map(triplet_part, gathered)
    totals = lax.psum(partial_sums, "site")
    triplet = (totals * float(LAT) ** (-1.5)).astype(jnp.bfloat16)
    comb_ids = jnp.arange(ncomb, dtype=jnp.int32)
    mom_ids = jnp.arange(nmom, dtype=jnp.int32)
    spin_ids = jnp.arange(nspin, dtype=jnp.int32)
    own_spins = lax.dynamic_slice_in_dim(spins, lax.axis_index("site") * comb_dev, comb_dev, 0)
    picker = (own_spins[:, :, None] == spin_ids[None, None, :]).astype(jnp.bfloat16)
    chosen = jnp.einsum(
        "cks,tsmn->tckmn", picker, perams, preferred_element_type=jnp.float32
    ).astype(jnp.bfloat16)
    first = jnp.einsum(
        "tijpk,tcmk->tcijpm", triplet, chosen[:, :, 2], preferred_element_type=jnp.float32
    ).astype(jnp.bfloat16)
    second = jnp.einsum(
        "tcmj,tcijpk->itcpmk", chosen[:, :, 1], first, preferred_element_type=jnp.float32
    ).astype(jnp.bfloat16)
    rows_sel = chosen[:, :, 0]
    cols_sel = lax.dynamic_slice_in_dim(rows_sel, first_mode, mode_dev, 3)
    own_blocks = lax.psum_scatter(
        jnp.einsum("tcmi,itcpjk->mtcpjk", cols_sel, second, preferred_element_type=jnp.float32),
        "mode",
        scatter_dimension=0,
        tiled=True,
    ).astype(jnp.bfloat16)
    all_blocks = lax.all_gather(own_blocks, "site", axis=2, tiled=True)
    swapped = lax.all_to_all(all_blocks, "mode", split_axis=4, concat_axis=0, tiled=True)
    pick_left = (
        (pair_combs[:, 0][:, None, None] == comb_ids[None, :, None])
        & (pair_moms[:, 0][:, None, None] == mom_ids[None, None, :])
    ).astype(jnp.bfloat16)
    pick_right = (
        (pair_combs[:, 1][:, None, None] == comb_ids[None, :, None])
        & (pair_moms[:, 1][:, None, None] == mom_ids[None, None, :])
    ).astype(jnp.bfloat16)
    left_block = jnp.einsum(
        "qcp,itcpjk->qtijk", pick_left, all_blocks, preferred_element_type=jnp.float32
    ).astype(jnp.bfloat16)
    right_block = jnp.einsum(
        "qcp,mtcpnk->qtmnk", pick_right, swapped, preferred_element_type=jnp.float32
    ).astype(jnp.bfloat16)
    partial_corr = jnp.einsum(
        "qtijk,qtjil->qtkl", left_block, right_block, preferred_element_type=jnp.float32
    ) * (1.0 / nmode)
    return lax.psum_scatter(
        partial_corr.astype(jnp.bfloat16), "mode", scatter_dimension=2, tiled=True
    ).astype(jnp.float32)


def solution(mesh):
    placed = (P(None, "mode", None, "site"), P(), P(), P(), P("site", None), P("site", None))
    return jax.shard_map(
        body, mesh=mesh, in_specs=placed, out_specs=P("site", None, "mode", None), check_vma=False
    )
```

profile of v0, /device:TPU:1, one launch (start us, length us, event | category | flops | bytes accessed | tf_op | source)
XLA Modules:
  0.0 597.3 jit_solution(13482562929319963017)
XLA Ops:
  6.5 2.0 copy.22
  8.7 0.9 dynamic-slice_reduce_fusion
  9.5 1.0 slice_reduce_fusion
  11.1 67.6 %all-gather.3.cloned.1.call-done = bf16[2,64,3,6912]{3,0,2,1:T(2,128)(2,1)} async-done(((bf16[2,4,3,6912]{3,0,2,1:T(2,128)(2,1)}), bf16[2,64,3,6912]{3,0,2,1:T(2,128)(2,1)}) %all-gather.3.cloned.1.call-update) | async-done | bytes 5308432 | tf_op jit(solution)/shard_map/all_gather | solution.py:30
  78.7 5.4 copy.23
  84.1 20.2 %while.13 = (s32[]{:T(128)}, f32[2,4,64,2,64]{4,2,3,1,0:T(8,128)S(1)}, bf16[2,64,3,6912]{3,1,2,0:T(8,128)(2,1)}, s32[]{:T(128)}, s32[6912]{0:T(1024)S(1)}, /*ind...) while((s32[]{:T(128)}, ...), condition=%wide.region_1.2_spmd.clone, body=%wide.region_0.1_spmd.clone.sunk | while | flops 1418867712 | bytes 57853072 | solution.py:52
  84.1 2.4 dynamic-slice_convert_fusion.3
  87.0 3.2 subtract_convert_fusion.4
  90.1 1.0 sine_add_fusion.2
  91.2 3.0 fusion.62
  94.2 2.4 dynamic-slice_convert_fusion.3
  97.1 3.2 subtract_convert_fusion.4
  100.2 1.0 sine_add_fusion.2
  101.3 3.0 fusion.62
  104.3 0.8 copy-done.2
  105.5 124.5 %all-reduce.3.cloned.1.call-done = f32[2,4,64,2,64]{4,2,3,1,0:T(8,128)} async-done(((f32[2,4,64,2,64]{4,2,3,1,0:T(8,128)}), f32[2,4,64,2,64]{4,2,3,1,0:T(8,128)}) %all-reduce.3.cloned.1.call-update) | async-done | bytes 262160 | tf_op jit(solution)/shard_map/psum | solution.py:53
  230.0 1.6 fusion.22
  231.8 4.9 convolution_bitcast_fusion
  236.7 9.1 %copy.26 = f32[64,2,1,2,64,64]{5,4,3,2,1,0:T(8,128)} copy(f32[64,2,1,2,64,64]{0,5,4,3,1,2:T(8,128)} %convolution_bitcast_fusion) | data formatting | bytes 8388608 | tf_op jit(solution)/shard_map/tcmi,itcpjk->mtcpjk/transpose | solution.py:72
  246.1 119.0 %reduce-scatter.3.cloned.1.call-done = f32[4,2,1,2,64,64]{5,4,3,2,1,0:T(8,128)} async-done(((f32[64,2,1,2,64,64]{5,4,3,2,1,0:T(8,128)}), f32[4,2,1,2,64,64]{5,4,3,2,1,0:T(8,128)}) %reduce-scatter.3.cloned.1.call-update) | async-done | bytes 262160 | tf_op jit(solution)/shard_map/reduce_scatter | solution.py:71
  365.0 1.8 convert_bitcast_fusion
  366.8 97.1 %all-gather.5.cloned.1.call-done = bf16[4,2,16,2,64,64]{5,4,3,1,0,2:T(8,128)(2,1)} async-done(((bf16[4,2,1,2,64,64]{5,4,3,1,0,2:T(8,128)(2,1)}), bf16[4,2,16,2,64,64]{5,4,3,1,0,2:T(8,128)(2,1)}) %all-gather.5.cloned.1.call-update) | async-done | bytes 2097168 | tf_op jit(solution)/shard_map/all_gather | solution.py:77
  464.0 6.9 %copy.74 = bf16[4,2,16,2,64,64]{5,2,3,1,0,4:T(8,128)(2,1)} copy(bf16[4,2,16,2,64,64]{5,4,3,1,0,2:T(8,128)(2,1)} %all-gather.5.cloned.1.call-done) | data formatting | bytes 4194304 | tf_op jit(solution)/shard_map/all_gather | solution.py:77
  470.8 7.6 %reshape.298 = bf16[16,2,32768]{2,1,0:T(2,128)(2,1)} reshape(bf16[64,4,2,2,16,64]{5,4,3,2,1,0:T(8,128)(2,1)} %bitcast.161) | data formatting | bytes 4194304
  478.4 9.6 %all-to-all-start = ((bf16[16,2,32768]{2,1,0:T(2,128)(2,1)}), bf16[16,2,32768]{2,1,0:T(2,128)(2,1)S(1)}, u32[]{:S(2)}, u32[]{:S(2)}) async-start(bf16[16,2,32768]{2,1,0:T(2,128)(2,1)} %reshape.298), calls=%async_computation.1 | async-start | bytes 4194304 | tf_op jit(solution)/shard_map/all_to_all | solution.py:78
  492.3 0.7 iota_compare_fusion.4
  493.1 3.4 multiply_reduce_fusion
  496.6 19.7 %all-to-all-done = bf16[16,2,32768]{2,1,0:T(2,128)(2,1)S(1)} async-done(((bf16[16,2,32768]{2,1,0:T(2,128)(2,1)}), bf16[16,2,32768]{2,1,0:T(2,128)(2,1)S(1)}, u32[]{:S(2)}, u32[]{:S(2)}) %all-to-all-start) | async-done | bytes 2097184 | tf_op jit(solution)/shard_map/all_to_all | solution.py:78
  516.3 5.0 reshape.299
  521.3 3.4 copy.30
  524.7 0.7 convolution_bitcast_fusion.1
  525.6 64.5 %all-reduce = bf16[1,2,64,64]{3,2,1,0:T(8,128)(2,1)S(1)} all-reduce(bf16[1,2,64,64]{3,2,1,0:T(8,128)(2,1)S(1)} %fusion.26), channel_id=3, replica_groups=mesh['mode'=16,'site'=16] {'mode'}, use_global_device_ids=true, to_apply=%region_4.5.clone | all-reduce | flops 8192 | bytes 32768
  (44 shorter events, 7.1 us)
Async XLA Ops:
  6.5 4.1 copy-start
  6.5 72.1 %all-gather.3.cloned.1.call-start = ((), (), s32[]{:S(2)}) async-start(), calls=%async_computation.2 | async-start | bytes 5640192 | tf_op jit(solution)/shard_map/all_gather | solution.py:30
  8.6 221.4 %all-reduce.3.cloned.1.call-start = ((), (), s32[]{:S(2)}) async-start(), calls=%async_computation.3 | async-start | bytes 1048576 | tf_op jit(solution)/shard_map/psum | solution.py:53
  104.3 0.8 copy-start.2
  105.1 259.9 %reduce-scatter.3.cloned.1.call-start = ((), (), s32[]{:S(2)}) async-start(), calls=%async_computation.4 | async-start | bytes 8912896 | tf_op jit(solution)/shard_map/reduce_scatter | solution.py:71
  245.8 218.1 %all-gather.5.cloned.1.call-start = ((), (), s32[]{:S(2)}) async-start(), calls=%async_computation.5 | async-start | bytes 4456448 | tf_op jit(solution)/shard_map/all_gather | solution.py:77
  470.8 17.1 %copy-start.5 = (u32[256]{0:T(256)S(1)}, u32[256]{0:T(256)}, u32[]{:S(2)}) copy-start(u32[256]{0:T(256)} %constant.88) | copy-start | bytes 3076
  470.8 18.4 %copy-start.3 = (s32[1,2]{1,0:T(1,128)S(1)}, s32[1,2]{1,0:T(1,128)}, u32[]{:S(2)}) copy-start(s32[1,2]{1,0:T(1,128)} %param.13) | copy-start | bytes 28
  470.8 19.6 %copy-start.4 = (s32[1,2]{1,0:T(1,128)S(1)}, s32[1,2]{1,0:T(1,128)}, u32[]{:S(2)}) copy-start(s32[1,2]{1,0:T(1,128)} %param.12) | copy-start | bytes 28
  478.4 37.9 %all-to-all-start = ((bf16[16,2,32768]{2,1,0:T(2,128)(2,1)}), bf16[16,2,32768]{2,1,0:T(2,128)(2,1)S(1)}, u32[]{:S(2)}, u32[]{:S(2)}) async-start(bf16[16,2,32768]{2,1,0:T(2,128)(2,1)} %reshape.298), calls=%async_computation.1 | async-start | bytes 4194304 | tf_op jit(solution)/shard_map/all_to_all | solution.py:78
  521.3 69.5 %copy-start.1 = (bf16[2,16,64,64]{3,2,1,0:T(8,128)(2,1)S(1)}, bf16[2,16,64,64]{3,2,1,0:T(8,128)(2,1)}, u32[]{:S(2)}) copy-start(bf16[2,16,64,64]{3,2,1,0:T(8,128)(2,1)} %param.9) | copy-start | bytes 786436
Sparse Core Ops, SparseCore 0:
  10.0 68.6 all-gather.2
  105.2 124.7 all-reduce.2
  245.9 119.0 reduce-scatter.2
  367.0 96.9 all-gather.4
where the time goes:
time: 602 us; the launch traced here: 597 us
  waiting for transfers between devices  428 us (71%)
  blocking collectives  64.5 us (11%)
  local copies, waits for them, and re-layouts  45.4 us (8%)
  other arithmetic  21.7 us (4%)
  between operations  13.9 us (2%)
  matrix products  13.8 us (2%)
  starting transfers between devices  9.87 us (2%)
    psum x1, waiting for transfers between devices, body(): totals = lax.psum(partial_sums, 'site')  124 us
    reduce_scatter x1, waiting for transfers between devices, body(): lax.psum_scatter(jnp.einsum('tcmi,itcpjk->mtcpjk', cols_sel, second, pref...  119 us
    all_gather x1, waiting for transfers between devices, body(): all_blocks = lax.all_gather(own_blocks, 'site', axis=2, tiled=True)  97.1 us
    all_gather x1, waiting for transfers between devices, body(): gathered = lax.all_gather(eigvecs, 'mode', axis=1, tiled=True)  67.6 us
    unnamed x1, blocking collectives  64.5 us
    unnamed x17, local copies, waits for them, and re-layouts  21.4 us
    all_to_all x1, waiting for transfers between devices, body(): lax.all_to_all(all_blocks, 'mode', split_axis=4, concat_axis=0, tiled=True)  19.7 us
  transfers between devices with their start and end apart: 5, of which 5 were waited for; matrix products, arithmetic and copies ran while one was open for 2% of the time, Pallas kernels for 0%

commit v1 on v0

v1 whole, which is shorter than its diff:
```python
import jax
import jax.numpy as jnp
import numpy as np
from jax import lax
from jax.experimental import pallas as pl
from jax.experimental.pallas import tpu as pltpu
from jax.sharding import PartitionSpec as P

LAT = 48
BLK = 8
NBLK = 8
PAIR_BASE = [64 * j * (j + 1) // 2 for j in range(NBLK + 1)]
NPAIR = PAIR_BASE[NBLK]
LANES = 8192
CHUNK = 1024


def roundup(x, m):
    return -(-x // m) * m


ROW_LEN = [PAIR_BASE[j + 1] for j in range(NBLK)]
ROW_OFF = np.concatenate([[0], np.cumsum([roundup(n, 128) for n in ROW_LEN])]).tolist()


def pair_modes():
    first, second = [], []
    for j in range(NBLK):
        width = BLK * (j + 1)
        for i in range(BLK):
            first += list(range(width))
            second += [BLK * j + i] * width
    return np.array([first, second], np.int32)


def segments():
    pieces = []
    for j in range(NBLK):
        done, total = 0, roundup(ROW_LEN[j], 128)
        while done < total:
            at = ROW_OFF[j] + done
            width = min(total - done, CHUNK - at % CHUNK)
            pieces.append((j, done, at // CHUNK, at % CHUNK, width))
            done += width
    return pieces


def nn(a, b):
    return lax.dot_general(a, b, (((1,), (0,)), ((), ())), preferred_element_type=jnp.float32)


def nt(a, b):
    return lax.dot_general(a, b, (((1,), (1,)), ((), ())), preferred_element_type=jnp.float32)


def tn(a, b):
    return lax.dot_general(a, b, (((0,), (0,)), ((), ())), preferred_element_type=jnp.float32)


def bf(x):
    return x.astype(jnp.bfloat16)


VMEM = pl.BlockSpec(memory_space=pltpu.VMEM)
SMEM = pl.BlockSpec(memory_space=pltpu.SMEM)


def split_kernel(x_ref, o_ref):
    peers, _, _, sites = o_ref.shape
    for t in range(x_ref.shape[0]):
        x = x_ref[t].astype(jnp.float32)
        rows = jnp.concatenate([x[m, c : c + 1] for c in range(3) for m in range(x.shape[0])], axis=0)
        for j in range(peers):
            o_ref[j, t] = bf(rows[:, j * sites : (j + 1) * sites])


def split_sites(x, peers):
    nslice, mode_dev, _, site_dev = x.shape
    return pl.pallas_call(
        split_kernel,
        out_shape=jax.ShapeDtypeStruct((peers, nslice, 3 * mode_dev, site_dev // peers), jnp.bfloat16),
        in_specs=[VMEM],
        out_specs=VMEM,
        name="split_sites",
    )(x)


def triplet_kernel(x_ref, phase_ref, o_ref, v_ref, w_ref, d_ref, r_ref):
    t = pl.program_id(0)
    peers, _, rows, sites = x_ref.shape
    mode_dev = rows // 3
    pad = v_ref.shape[2]
    for c in range(3):
        v_ref[c, :, pad - 128 :] = jnp.zeros((v_ref.shape[1], 128), jnp.float32)
        v_ref[c, :, :sites] = jnp.concatenate(
            [x_ref[i, 0].astype(jnp.float32)[c * mode_dev : (c + 1) * mode_dev] for i in range(peers)], axis=0
        )
    for c in range(3):
        v = v_ref[c]
        w = jnp.concatenate(
            [v[BLK * j : BLK * (j + 1)] * phase_ref[p : p + 1] for j in range(NBLK) for p in range(2)], axis=0
        )
        w_ref[c * pad : (c + 1) * pad] = bf(w.T)
    for j in range(NBLK):
        width = BLK * (j + 1)
        for i in range(0, BLK, 2):
            for c in range(3):
                c1, c2 = (c + 1) % 3, (c + 2) % 3
                cross = jnp.concatenate(
                    [
                        v_ref[c1, :width] * v_ref[c2, n : n + 1] - v_ref[c2, :width] * v_ref[c1, n : n + 1]
                        for n in (BLK * j + i, BLK * j + i + 1)
                    ],
                    axis=0,
                )
                d_ref[i * width : (i + 2) * width, c * pad : (c + 1) * pad] = bf(cross)
        part = nn(d_ref[: BLK * width], w_ref[...])
        r_ref[:, PAIR_BASE[j] : PAIR_BASE[j + 1]] = part.T
    for j, pair, chunk, lane, width in segments():
        o_ref[chunk, :, lane : lane + width] = bf(r_ref[2 * BLK * j : 2 * BLK * (j + 1), pair : pair + width])
    used = ROW_OFF[NBLK] % CHUNK
    o_ref[LANES // CHUNK - 1, :, used:] = jnp.zeros((2 * BLK, CHUNK - used), jnp.bfloat16)


def triplet_parts(x, phase):
    peers, nslice, rows, sites = x.shape
    nmode = peers * rows // 3
    pad = phase.shape[1]
    chunks = LANES // CHUNK
    return pl.pallas_call(
        triplet_kernel,
        grid=(nslice,),
        out_shape=jax.ShapeDtypeStruct((nslice * chunks, 2 * BLK, CHUNK), jnp.bfloat16),
        in_specs=[
            pl.BlockSpec((peers, 1, rows, sites), lambda t: (0, t, 0, 0)),
            pl.BlockSpec((2, pad), lambda t: (0, 0)),
        ],
        out_specs=pl.BlockSpec((chunks, 2 * BLK, CHUNK), lambda t: (t, 0, 0)),
        scratch_shapes=[
            pltpu.VMEM((3, nmode, pad), jnp.float32),
            pltpu.VMEM((3 * pad, 2 * nmode), jnp.bfloat16),
            pltpu.VMEM((BLK * nmode, 3 * pad), jnp.bfloat16),
            pltpu.VMEM((2 * nmode, NPAIR), jnp.float32),
        ],
        name="triplet_parts",
    )(x, phase)


def sum_kernel(scale, x_ref, o_ref):
    total = x_ref[0].astype(jnp.float32)
    for i in range(1, x_ref.shape[0]):
        total = total + x_ref[i].astype(jnp.float32)
    total = bf(total * scale)
    for i in range(o_ref.shape[0]):
        o_ref[i] = total


def sum_and_repeat(x, copies, scale):
    def kernel(x_ref, o_ref):
        sum_kernel(scale, x_ref, o_ref)

    return pl.pallas_call(
        kernel,
        out_shape=jax.ShapeDtypeStruct((copies,) + x.shape[1:], jnp.bfloat16),
        in_specs=[VMEM],
        out_specs=VMEM,
        name="sum_and_repeat",
    )(x)


def exchange_kernel(spins_ref, combs_ref, moms_ref, own_ref, tri_ref, per_ref, modes_ref, o_ref, u_ref):
    nmode = per_ref.shape[-1]
    rows_out = o_ref.shape[2]
    spin_a = [spins_ref[combs_ref[0, 0], i] for i in range(3)]
    spin_b = [spins_ref[combs_ref[0, 1], i] for i in range(3)]
    low, mid = modes_ref[0:1], modes_ref[1:2]
    row = lax.broadcasted_iota(jnp.int32, (nmode, NPAIR), 0)
    is_low, is_mid = row == low, row == mid
    one, zero = jnp.float32(1), jnp.float32(0)
    sel_low, sel_mid = bf(jnp.where(is_low, one, zero)), bf(jnp.where(is_mid, one, zero))
    ordered = (low < mid) & (mid < row)
    own_row = lax.broadcasted_iota(jnp.int32, (8, nmode), 0)
    own_col = lax.broadcasted_iota(jnp.int32, (8, nmode), 1)
    own = bf(jnp.where((own_col == own_row + own_ref[0, 0]) & (own_row < rows_out), one, zero))

    def slices(t, carry):
        for j, pair, chunk, lane, width in segments():
            both = tri_ref[t * (LANES // CHUNK) + chunk, :, lane : lane + width].astype(jnp.float32)
            for side in range(2):
                picked = jnp.where(moms_ref[0, side] == 0, both[:BLK], both[BLK:])
                u_ref[side, BLK * j : BLK * (j + 1), pair : pair + width] = picked
        tri_a = jnp.where(ordered, u_ref[0], zero)
        tri_b = jnp.where(ordered, u_ref[1], zero)
        p1a, p2a, p3a = [per_ref[t, s] for s in spin_a]
        p1b, p2b, p3b = [per_ref[t, s] for s in spin_b]
        q = bf(nn(own, p3a))
        q_low, q_mid = nn(q, sel_low), nn(q, sel_mid)
        pairs = nn(q, bf(tri_a))
        to_mid = jnp.concatenate(
            [bf(jnp.where(is_low, pairs[k : k + 1], -tri_a * q_low[k : k + 1])) for k in range(rows_out)], axis=0
        )
        to_low = jnp.concatenate([bf(tri_a * q_mid[k : k + 1]) for k in range(rows_out)], axis=0)
        half = nt(to_mid, sel_mid) + nt(to_low, sel_low)
        cut = lambda x, k: x[k * nmode : (k + 1) * nmode]
        anti = [cut(half, k) - cut(half, k).T for k in range(rows_out)]
        right = bf(nt(bf(jnp.concatenate(anti, axis=0)), p2a))
        block = jnp.concatenate([bf(nn(p1a, cut(right, k))) for k in range(rows_out)], axis=0)
        turned = bf(nn(block, p1b))
        back = [tn(p2b, cut(turned, k)) for k in range(rows_out)]
        weight = bf(jnp.concatenate([x.T - x for x in back], axis=0))
        at_low, at_mid = nn(weight, sel_low), nn(weight, sel_mid)
        fill = jnp.zeros((8 - rows_out, NPAIR), jnp.float32)

        def stack(f):
            return bf(jnp.concatenate([jnp.sum(f(k), axis=0, keepdims=True) for k in range(rows_out)] + [fill], axis=0))

        on_high = stack(lambda k: jnp.where(is_mid, cut(at_low, k), zero))
        on_mid = stack(lambda k: cut(at_low, k) * tri_b)
        on_low = stack(lambda k: cut(at_mid, k) * tri_b)
        ends = nt(on_mid, sel_mid) - nt(on_low, sel_low) - nt(on_high, bf(tri_b))
        head = bf(ends)
        tail = bf(ends - head.astype(jnp.float32))
        o_ref[0, t] = ((nt(head, p3b) + nt(tail, p3b)) * (1.0 / nmode))[:rows_out]
        return carry

    lax.fori_loop(0, o_ref.shape[1], slices, 0)


def exchange_rows(spins, pair_combs, pair_moms, own, triplets, perams, rows_out):
    nslice, _, nmode, _ = perams.shape
    return pl.pallas_call(
        exchange_kernel,
        out_shape=jax.ShapeDtypeStruct((1, nslice, rows_out, nmode), jnp.float32),
        in_specs=[SMEM, SMEM, SMEM, SMEM, VMEM, VMEM, VMEM],
        out_specs=VMEM,
        scratch_shapes=[pltpu.VMEM((2, nmode, NPAIR), jnp.float32)],
        name="exchange_rows",
    )(spins, pair_combs, pair_moms, own, triplets, perams, jnp.asarray(pair_modes()))


def hartley(momenta, glob):
    coord_x = glob // (LAT * LAT)
    coord_y = glob // LAT % LAT
    coord_z = glob % LAT
    wave = (
        momenta[:, 0:1] * coord_x[None]
        + momenta[:, 1:2] * coord_y[None]
        + momenta[:, 2:3] * coord_z[None]
    ) % LAT
    theta = wave.astype(jnp.float32) * (2.0 * jnp.pi / LAT)
    return jnp.cos(theta) + jnp.sin(theta)


def swap(x, axis):
    return lax.all_to_all(x, axis, split_axis=0, concat_axis=0)


def body(eigvecs, perams, momenta, spins, pair_combs, pair_moms):
    nslice, mode_dev, _, site_dev = eigvecs.shape
    peers = lax.axis_size("mode")
    sites = site_dev // peers
    mode_id = lax.axis_index("mode")
    start = lax.axis_index("site") * site_dev + mode_id * sites
    phase = hartley(momenta, start + jnp.arange(roundup(sites, 128), dtype=jnp.int32))
    vectors = swap(split_sites(eigvecs, peers), "mode")
    parts = swap(triplet_parts(vectors, phase), "mode")
    parts = swap(sum_and_repeat(parts, lax.axis_size("site"), 1.0), "site")
    triplets = swap(sum_and_repeat(parts, peers, float(LAT) ** (-1.5)), "mode")
    own = (mode_id * mode_dev).reshape(1, 1).astype(jnp.int32)
    return exchange_rows(spins, pair_combs, pair_moms, own, triplets, perams, mode_dev)


def solution(mesh):
    placed = (P(None, "mode", None, "site"), P(), P(), P(), P("site", None), P("site", None))
    return jax.shard_map(
        body, mesh=mesh, in_specs=placed, out_specs=P("site", None, "mode", None), check_vma=False
    )
```

time: 602 us -> 107 us (0.18)
  waiting for transfers between devices: 428 us -> 19.3 us
  local copies, waits for them, and re-layouts: 45.4 us -> 6.66 us
  blocking collectives: 64.5 us -> 40.3 us
  Pallas kernels: 0 us -> 23.1 us
  other arithmetic: 21.7 us -> 0.79 us
  between operations: 13.9 us -> 0.03 us
  matrix products: 13.8 us -> 0 us
  starting transfers between devices: 9.87 us -> 16.1 us
    all_gather x2 -> x0, waiting for transfers between devices: 165 us -> none  [the longest x1 97.1 us: body(): all_blocks = lax.all_gather(own_blocks, 'site', axis=2, tiled=True)]
    psum x1 -> x0, waiting for transfers between devices: 124 us -> none  [body(): totals = lax.psum(partial_sums, 'site')]
    reduce_scatter x1 -> x0, waiting for transfers between devices: 119 us -> none  [body(): lax.psum_scatter(jnp.einsum('tcmi,itcpjk->mtcpjk', cols_sel, second, pref...]
    unnamed x1 -> x0, blocking collectives: 64.5 us -> none
    all_to_all x0 -> x2, blocking collectives: none -> 40.3 us  [swap(): return lax.all_to_all(x, axis, split_axis=0, concat_axis=0)]
    pallas_call x0 -> x5, Pallas kernels: none -> 23.1 us  [the longest x1 9.86 us: exchange_rows(): pl.pallas_call(exchange_kernel, out_shape=jax.ShapeDtypeStruct((1, nslice...]
    unnamed x17 -> x8, local copies, waits for them, and re-layouts: 21.4 us -> 3.38 us
    dot_general x7 -> x0, matrix products: 13.8 us -> none  [the longest x2 5.98 us: triplet_part(): lax.dot_general(diquark.reshape(mode_dev * nmode, 3 * site_dev), weighted...]
  transfers between devices with their start and end apart: 5 -> 2, of which waited for: 5 -> 2; matrix products, arithmetic and copies ran while one was open for 2% -> 2% of each run, Pallas kernels for 0% -> 0%
where the time goes in v1:
time: 107 us; the launch traced here: 106 us
  blocking collectives  40.3 us (38%)
  Pallas kernels  23.1 us (22%)
  waiting for transfers between devices  19.3 us (18%)
  starting transfers between devices  16.1 us (15%)
  local copies, waits for them, and re-layouts  6.66 us (6%)
    all_to_all x2, blocking collectives, swap(): return lax.all_to_all(x, axis, split_axis=0, concat_axis=0)  40.3 us
    all_to_all x2, waiting for transfers between devices, swap(): return lax.all_to_all(x, axis, split_axis=0, concat_axis=0)  19.3 us
    all_to_all x2, starting transfers between devices, swap(): return lax.all_to_all(x, axis, split_axis=0, concat_axis=0)  16.1 us
    pallas_call x1, Pallas kernels, exchange_rows(): pl.pallas_call(exchange_kernel, out_shape=jax.ShapeDtypeStruct((1, nslice...  9.86 us
    pallas_call x1, Pallas kernels, triplet_parts(): pl.pallas_call(triplet_kernel, grid=(nslice,), out_shape=jax.ShapeDtypeSt...  7.09 us
    pallas_call x2, Pallas kernels, sum_and_repeat(): pl.pallas_call(kernel, out_shape=jax.ShapeDtypeStruct((copies,) + x.shape...  3.84 us
    unnamed x8, local copies, waits for them, and re-layouts  3.38 us
    pallas_call x1, Pallas kernels, split_sites(): pl.pallas_call(split_kernel, out_shape=jax.ShapeDtypeStruct((peers, nslic...  2.25 us
  transfers between devices with their start and end apart: 2, of which 2 were waited for; matrix products, arithmetic and copies ran while one was open for 2% of the time, Pallas kernels for 0%

profile of v1, /device:TPU:1, one launch (start us, length us, event | category | flops | bytes accessed | tf_op | source)
XLA Modules:
  0.0 106.2 jit_solution(5436584744883691463)
XLA Ops:
  0.0 1.9 %copy.10.x_ref = bf16[2,4,3,6912]{3,2,1,0:T(4,128)(2,1)} copy(bf16[2,4,3,6912]{3,1,2,0:T(4,128)(2,1)} %param.7) | data formatting | bytes 663552 | tf_op args[0]
  1.9 2.3 %split_sites.1 = bf16[16,2,12,432]{3,2,1,0:T(8,128)(2,1)} custom-call(bf16[2,4,3,6912]{3,2,1,0:T(4,128)(2,1)} %copy.10.x_ref), custom_call_target="tpu_custom_call" | custom-call | tf_op jit(solution)/shard_map/split_sites/pallas_call | solution.py:79
  4.2 2.2 %copy.11 = bf16[16,2,12,432]{3,1,2,0:T(2,128)(2,1)} copy(bf16[16,2,12,432]{3,2,1,0:T(8,128)(2,1)} %split_sites.1) | data formatting | bytes 663552 | tf_op jit(solution)/shard_map/split_sites/pallas_call | solution.py:79
  6.4 0.0 copy-start.1
  6.4 8.6 %all-to-all-start = ((bf16[16,2,12,432]{3,1,2,0:T(2,128)(2,1)}), bf16[16,2,12,432]{3,1,2,0:T(2,128)(2,1)S(1)}, u32[]{:S(2)}, u32[]{:S(2)}) async-start(bf16[16,2,12,432]{3,1,2,0:T(2,128)(2,1)} %copy.11), calls=%async_computation | async-start | bytes 786432 | tf_op jit(solution)/shard_map/all_to_all | solution.py:255
  15.0 0.0 copy-done.1
  15.0 0.2 slice_reduce_fusion.2
  15.2 0.8 sine_add_fusion.phase_ref
  15.9 8.8 %all-to-all-done = bf16[16,2,12,432]{3,1,2,0:T(2,128)(2,1)S(1)} async-done(((bf16[16,2,12,432]{3,1,2,0:T(2,128)(2,1)}), bf16[16,2,12,432]{3,1,2,0:T(2,128)(2,1)S(1)}, u32[]{:S(2)}, u32[]{:S(2)}) %all-to-all-start) | async-done | bytes 331808 | tf_op jit(solution)/shard_map/all_to_all | solution.py:255
  24.7 0.9 copy.12.x_ref
  25.6 7.1 %triplet_parts.1 = bf16[16,16,1024]{2,1,0:T(8,128)(2,1)} custom-call(bf16[16,2,12,432]{3,2,1,0:T(8,128)(2,1)} %copy.12.x_ref, f32[2,512]{1,0:T(2,128)} %sine_add_fusion.phase_ref), custom_call_target="tpu_custom_call" | custom-call | tf_op jit(solution)/shard_map/triplet_parts/pallas_call | solution.py:130
  32.7 16.6 %all_to_all.20.x_ref = bf16[16,16,1024]{2,1,0:T(8,128)(2,1)} all-to-all(bf16[16,16,1024]{2,1,0:T(8,128)(2,1)} %triplet_parts.1), channel_id=1, replica_groups=mesh['mode'=16,'site'=16] {'mode'}, dimensions={0} | all-to-all | bytes 1048576 | tf_op jit(solution)/shard_map/all_to_all | solution.py:255
  49.3 1.9 %sum_and_repeat.2 = bf16[16,16,1024]{2,1,0:T(8,128)(2,1)} custom-call(bf16[16,16,1024]{2,1,0:T(8,128)(2,1)} %all_to_all.20.x_ref), custom_call_target="tpu_custom_call" | custom-call | tf_op jit(solution)/shard_map/sum_and_repeat/pallas_call | solution.py:162
  51.2 23.7 %all_to_all.21.x_ref = bf16[16,16,1024]{2,1,0:T(8,128)(2,1)} all-to-all(bf16[16,16,1024]{2,1,0:T(8,128)(2,1)} %sum_and_repeat.2), channel_id=1, replica_groups=mesh['mode'=16,'site'=16] {'site'}, dimensions={0} | all-to-all | bytes 1048576 | tf_op jit(solution)/shard_map/all_to_all | solution.py:255
  74.9 1.9 %sum_and_repeat.3 = bf16[16,16,1024]{2,1,0:T(8,128)(2,1)} custom-call(bf16[16,16,1024]{2,1,0:T(8,128)(2,1)} %all_to_all.21.x_ref), custom_call_target="tpu_custom_call" | custom-call | tf_op jit(solution)/shard_map/sum_and_repeat/pallas_call | solution.py:162
  76.9 0.0 copy-start.2
  76.9 7.5 %all-to-all-start.3 = ((bf16[16,16,1024]{2,1,0:T(8,128)(2,1)}), bf16[16,16,1024]{2,1,0:T(8,128)(2,1)S(1)}, u32[]{:S(2)}, u32[]{:S(2)}) async-start(bf16[16,16,1024]{2,1,0:T(8,128)(2,1)} %sum_and_repeat.3), calls=%async_computation.3 | async-start | bytes 1048576 | tf_op jit(solution)/shard_map/all_to_all | solution.py:255
  84.4 0.0 copy-done.2
  84.4 0.7 copy.13.spins_ref
  85.1 10.5 %all-to-all-done.3.tri_ref = bf16[16,16,1024]{2,1,0:T(8,128)(2,1)S(1)} async-done(((bf16[16,16,1024]{2,1,0:T(8,128)(2,1)}), bf16[16,16,1024]{2,1,0:T(8,128)(2,1)S(1)}, u32[]{:S(2)}, u32[]{:S(2)}) %all-to-all-start.3) | async-done | bytes 524320 | tf_op jit(solution)/shard_map/all_to_all | solution.py:255
  95.6 0.0 copy-start
  95.6 0.8 copy-done
  96.3 9.9 %exchange_rows.1 = f32[1,2,4,64]{3,2,1,0:T(4,128)} custom-call(s32[16,3]{1,0:T(8,128)} %copy.13.spins_ref, s32[1,2]{1,0:T(1,128)} %combs_ref.1, s32[1,2]{1,0:T(1,128)} %moms_ref.1, s32[1,1]{1,0:T(1,128)} %bitcast.own_ref, bf16[16,16,1024]{2,1,0:T(8,128)(2,1)} %copy-done, bf16[2,16,64,64]{3,2,1,0:T(8,128)(2,1)} %per_ref.1, s32[2,2304]{1,0:T(2,128)} %constant.52.clone.modes_ref), custom_call_target="tpu_custom_call" | custom-call | tf_op jit(solution)/shard_map/exchange_rows/pallas_call | solution.py:231
  (2 shorter events, 0.0 us)
Async XLA Ops:
  6.4 8.6 %copy-start.1 = (s32[2,3]{1,0:T(2,128)S(1)}, s32[2,3]{1,0:T(2,128)}, u32[]{:S(2)}) copy-start(s32[2,3]{1,0:T(2,128)} %param.9) | copy-start | bytes 76
  6.4 18.3 %all-to-all-start = ((bf16[16,2,12,432]{3,1,2,0:T(2,128)(2,1)}), bf16[16,2,12,432]{3,1,2,0:T(2,128)(2,1)S(1)}, u32[]{:S(2)}, u32[]{:S(2)}) async-start(bf16[16,2,12,432]{3,1,2,0:T(2,128)(2,1)} %copy.11), calls=%async_computation | async-start | bytes 786432 | tf_op jit(solution)/shard_map/all_to_all | solution.py:255
  76.9 7.5 %copy-start.2 = (s32[16,3]{0,1:T(4,128)S(1)}, s32[16,3]{0,1:T(4,128)}, u32[]{:S(2)}) copy-start(s32[16,3]{0,1:T(4,128)} %param.10) | copy-start | bytes 580
  76.9 18.7 %all-to-all-start.3 = ((bf16[16,16,1024]{2,1,0:T(8,128)(2,1)}), bf16[16,16,1024]{2,1,0:T(8,128)(2,1)S(1)}, u32[]{:S(2)}, u32[]{:S(2)}) async-start(bf16[16,16,1024]{2,1,0:T(8,128)(2,1)} %sum_and_repeat.3), calls=%async_computation.3 | async-start | bytes 1048576 | tf_op jit(solution)/shard_map/all_to_all | solution.py:255
  95.6 0.8 copy-start

commit v2 on v1

v2 whole, which is shorter than its diff:
```python
import jax
import jax.numpy as jnp
import numpy as np
from jax import lax
from jax.experimental import pallas as pl
from jax.experimental.pallas import tpu as pltpu
from jax.sharding import Mesh
from jax.sharding import PartitionSpec as P

LAT = 48
BLK = 8
NBLK = 8
PAIR_BASE = [64 * j * (j + 1) // 2 for j in range(NBLK + 1)]
NPAIR = PAIR_BASE[NBLK]
LANES = 8192
CHUNK = 512


def roundup(x, m):
    return -(-x // m) * m


ROW_LEN = [PAIR_BASE[j + 1] for j in range(NBLK)]
ROW_OFF = np.concatenate([[0], np.cumsum([roundup(n, 128) for n in ROW_LEN])]).tolist()


def pair_modes():
    first, second = [], []
    for j in range(NBLK):
        width = BLK * (j + 1)
        for i in range(BLK):
            first += list(range(width))
            second += [BLK * j + i] * width
    return np.array([first, second], np.int32)


def segments():
    pieces = []
    for j in range(NBLK):
        done, total = 0, roundup(ROW_LEN[j], 128)
        while done < total:
            at = ROW_OFF[j] + done
            width = min(total - done, CHUNK - at % CHUNK)
            pieces.append((j, done, at // CHUNK, at % CHUNK, width))
            done += width
    return pieces


def nn(a, b):
    return lax.dot_general(a, b, (((1,), (0,)), ((), ())), preferred_element_type=jnp.float32)


def nt(a, b):
    return lax.dot_general(a, b, (((1,), (1,)), ((), ())), preferred_element_type=jnp.float32)


def tn(a, b):
    return lax.dot_general(a, b, (((0,), (0,)), ((), ())), preferred_element_type=jnp.float32)


def bf(x):
    return x.astype(jnp.bfloat16)


VMEM = pl.BlockSpec(memory_space=pltpu.VMEM)
SMEM = pl.BlockSpec(memory_space=pltpu.SMEM)

MODE = ("x_hi", "y", "core")
SITE = ("z", "x_lo")
PLANE = ("x_hi", "y", "core", "x_lo")


def on_chip(x):
    return pltpu.with_memory_space_constraint(x, pltpu.VMEM)


def split_kernel(x_ref, o_ref):
    peers, _, sites = o_ref.shape
    nslice, ncolor, mode_dev, _ = x_ref.shape
    x = jnp.concatenate([x_ref[t, c].astype(jnp.float32) for t in range(nslice) for c in range(ncolor)], axis=0)
    for j in range(peers):
        o_ref[j] = bf(x[:, j * sites : (j + 1) * sites])


def split_sites(x, peers):
    nslice, ncolor, mode_dev, site_dev = x.shape
    return pl.pallas_call(
        split_kernel,
        out_shape=pltpu.VMEM((peers, nslice * ncolor * mode_dev, site_dev // peers), jnp.bfloat16),
        in_specs=[VMEM],
        out_specs=VMEM,
        name="split_sites",
    )(x)


def triplet_kernel(x_ref, phase_ref, o_ref, v_ref, w_ref, d_ref, r_ref):
    nslice, ncolor, nmode, pad = v_ref.shape
    peers, rows, sites = x_ref.shape
    mode_dev = nmode // peers
    x = [x_ref[i].astype(jnp.float32) for i in range(peers)]
    for t in range(nslice):
        for c in range(ncolor):
            at = (t * ncolor + c) * mode_dev
            v_ref[t, c, :, pad - 128 :] = jnp.zeros((nmode, 128), jnp.float32)
            v_ref[t, c, :, :sites] = jnp.concatenate([y[at : at + mode_dev] for y in x], axis=0)

    def one_slice(t, carry):
        for c in range(ncolor):
            v = v_ref[t, c]
            w = jnp.concatenate(
                [v[BLK * j : BLK * (j + 1)] * phase_ref[p : p + 1] for j in range(NBLK) for p in range(2)], axis=0
            )
            w_ref[c * pad : (c + 1) * pad] = bf(w.T)
        for j in range(NBLK):
            width = BLK * (j + 1)
            for i in range(0, BLK, 2):
                for c in range(ncolor):
                    c1, c2 = (c + 1) % ncolor, (c + 2) % ncolor
                    cross = jnp.concatenate(
                        [
                            v_ref[t, c1, :width] * v_ref[t, c2, n : n + 1]
                            - v_ref[t, c2, :width] * v_ref[t, c1, n : n + 1]
                            for n in (BLK * j + i, BLK * j + i + 1)
                        ],
                        axis=0,
                    )
                    d_ref[i * width : (i + 2) * width, c * pad : (c + 1) * pad] = bf(cross)
            part = nn(d_ref[: BLK * width], w_ref[...])
            r_ref[:, PAIR_BASE[j] : PAIR_BASE[j + 1]] = part.T
        first = t * (LANES // CHUNK)
        for j, pair, chunk, lane, width in segments():
            o_ref[first + chunk, :, lane : lane + width] = bf(
                r_ref[2 * BLK * j : 2 * BLK * (j + 1), pair : pair + width]
            )
        used = ROW_OFF[NBLK] % CHUNK
        o_ref[first + LANES // CHUNK - 1, :, used:] = jnp.zeros((2 * BLK, CHUNK - used), jnp.bfloat16)
        return carry

    lax.fori_loop(0, nslice, one_slice, 0)


def triplet_parts(x, phase, nslice):
    peers, rows, sites = x.shape
    mode_dev = rows // (3 * nslice)
    nmode = peers * mode_dev
    pad = phase.shape[1]
    return pl.pallas_call(
        triplet_kernel,
        out_shape=pltpu.VMEM((nslice * LANES // CHUNK, 2 * BLK, CHUNK), jnp.bfloat16),
        in_specs=[VMEM, VMEM],
        out_specs=VMEM,
        scratch_shapes=[
            pltpu.VMEM((nslice, 3, nmode, pad), jnp.float32),
            pltpu.VMEM((3 * pad, 2 * nmode), jnp.bfloat16),
            pltpu.VMEM((BLK * nmode, 3 * pad), jnp.bfloat16),
            pltpu.VMEM((2 * nmode, NPAIR), jnp.float32),
        ],
        name="triplet_parts",
    )(on_chip(x), on_chip(phase))


def sum_kernel(scale, x_ref, o_ref):
    total = x_ref[0].astype(jnp.float32)
    for i in range(1, x_ref.shape[0]):
        total = total + x_ref[i].astype(jnp.float32)
    total = bf(total * scale)
    for i in range(o_ref.shape[0]):
        o_ref[i] = total


def sum_and_repeat(x, copies, scale):
    def kernel(x_ref, o_ref):
        sum_kernel(scale, x_ref, o_ref)

    return pl.pallas_call(
        kernel,
        out_shape=pltpu.VMEM((copies,) + x.shape[1:], jnp.bfloat16),
        in_specs=[VMEM],
        out_specs=VMEM,
        name="sum_and_repeat",
    )(on_chip(x))


def exchange_kernel(spins_ref, combs_ref, moms_ref, own_ref, tri_ref, per_ref, modes_ref, o_ref, u_ref):
    nmode = per_ref.shape[-1]
    slices, rows_out = range(o_ref.shape[1]), o_ref.shape[2]
    spin_a = [spins_ref[combs_ref[0, 0], i] for i in range(3)]
    spin_b = [spins_ref[combs_ref[0, 1], i] for i in range(3)]
    low, mid = modes_ref[0:1], modes_ref[1:2]
    row = lax.broadcasted_iota(jnp.int32, (nmode, NPAIR), 0)
    is_low, is_mid = row == low, row == mid
    one, zero = jnp.float32(1), jnp.float32(0)
    sel_low, sel_mid = bf(jnp.where(is_low, one, zero)), bf(jnp.where(is_mid, one, zero))
    ordered = (low < mid) & (mid < row)
    own_row = lax.broadcasted_iota(jnp.int32, (8, nmode), 0)
    own_col = lax.broadcasted_iota(jnp.int32, (8, nmode), 1)
    own = bf(jnp.where((own_col == own_row + own_ref[0, 0]) & (own_row < rows_out), one, zero))
    stack = lambda xs: jnp.concatenate(list(xs), axis=0)
    cut = lambda x, i: x[i * nmode : (i + 1) * nmode]
    each = [(t, k, t * rows_out + k) for t in slices for k in range(rows_out)]
    for t in slices:
        for j, pair, chunk, lane, width in segments():
            both = tri_ref[t * (LANES // CHUNK) + chunk, :, lane : lane + width].astype(jnp.float32)
            for side in range(2):
                picked = jnp.where(moms_ref[0, side] == 0, both[:BLK], both[BLK:])
                u_ref[t, side, BLK * j : BLK * (j + 1), pair : pair + width] = picked
    tri_a = [jnp.where(ordered, u_ref[t, 0], zero) for t in slices]
    tri_b = [jnp.where(ordered, u_ref[t, 1], zero) for t in slices]
    mats_a = [[per_ref[t, s] for s in spin_a] for t in slices]
    mats_b = [[per_ref[t, s] for s in spin_b] for t in slices]
    q = bf(stack(nn(own, mats_a[t][2]) for t in slices))
    q_low, q_mid = nn(q, sel_low), nn(q, sel_mid)
    pairs = [nn(q[8 * t : 8 * t + 8], bf(tri_a[t])) for t in slices]
    line = lambda x, t, k: x[8 * t + k : 8 * t + k + 1]
    to_mid = stack(bf(jnp.where(is_low, pairs[t][k : k + 1], -tri_a[t] * line(q_low, t, k))) for t, k, _ in each)
    to_low = stack(bf(tri_a[t] * line(q_mid, t, k)) for t, k, _ in each)
    half = nt(to_mid, sel_mid) + nt(to_low, sel_low)
    anti = [bf(cut(half, i) - cut(half, i).T) for _, _, i in each]
    size = rows_out * nmode
    right = [bf(nt(stack(anti[t * rows_out : (t + 1) * rows_out]), mats_a[t][1])) for t in slices]
    block = [stack(bf(nn(mats_a[t][0], cut(right[t], k))) for k in range(rows_out)) for t in slices]
    turned = [bf(nn(block[t], mats_b[t][0])) for t in slices]
    back = [tn(mats_b[t][1], cut(turned[t], k)) for t, k, _ in each]
    weight = bf(stack(x.T - x for x in back))
    at_low, at_mid = nn(weight, sel_low), nn(weight, sel_mid)
    fill = [jnp.zeros((8 - rows_out, NPAIR), jnp.float32)]

    def summed(f):
        return [
            bf(stack([jnp.sum(f(t, t * rows_out + k), axis=0, keepdims=True) for k in range(rows_out)] + fill))
            for t in slices
        ]

    on_high = summed(lambda t, i: jnp.where(is_mid, cut(at_low, i), zero))
    on_mid = stack(summed(lambda t, i: cut(at_low, i) * tri_b[t]))
    on_low = stack(summed(lambda t, i: cut(at_mid, i) * tri_b[t]))
    ends = nt(on_mid, sel_mid) - nt(on_low, sel_low) - stack(nt(on_high[t], bf(tri_b[t])) for t in slices)
    head = bf(ends)
    tail = bf(ends - head.astype(jnp.float32))
    for t in slices:
        mat, own_rows = mats_b[t][2], slice(8 * t, 8 * t + 8)
        o_ref[0, t] = ((nt(head[own_rows], mat) + nt(tail[own_rows], mat)) * (1.0 / nmode))[:rows_out]


def exchange_rows(spins, pair_combs, pair_moms, own, triplets, perams, rows_out):
    nslice, _, nmode, _ = perams.shape
    return pl.pallas_call(
        exchange_kernel,
        out_shape=jax.ShapeDtypeStruct((1, nslice, rows_out, nmode), jnp.float32),
        in_specs=[SMEM, SMEM, SMEM, SMEM, VMEM, VMEM, VMEM],
        out_specs=VMEM,
        scratch_shapes=[pltpu.VMEM((nslice, 2, nmode, NPAIR), jnp.float32)],
        name="exchange_rows",
    )(spins, pair_combs, pair_moms, own, on_chip(triplets), on_chip(perams), jnp.asarray(pair_modes()))


def hartley(momenta, glob):
    coord_x = glob // (LAT * LAT)
    coord_y = glob // LAT % LAT
    coord_z = glob % LAT
    wave = (
        momenta[:, 0:1] * coord_x[None]
        + momenta[:, 1:2] * coord_y[None]
        + momenta[:, 2:3] * coord_z[None]
    ) % LAT
    theta = wave.astype(jnp.float32) * (2.0 * jnp.pi / LAT)
    return jnp.cos(theta) + jnp.sin(theta)


def swap(x, axis):
    return lax.all_to_all(x, axis, split_axis=0, concat_axis=0)


def body(eigvecs, perams, momenta, spins, pair_combs, pair_moms):
    nslice, mode_dev, _, site_dev = eigvecs.shape
    peers = lax.axis_size(MODE)
    sites = site_dev // peers
    mode_id = lax.axis_index(MODE)
    start = lax.axis_index(SITE) * site_dev + mode_id * sites
    phase = hartley(momenta, start + jnp.arange(roundup(sites, 128), dtype=jnp.int32))
    vectors = swap(split_sites(eigvecs.transpose(0, 2, 1, 3), peers), MODE)
    parts = swap(triplet_parts(vectors, phase, nslice), PLANE)
    parts = swap(sum_and_repeat(parts, lax.axis_size("z"), 1.0), "z")
    triplets = swap(sum_and_repeat(parts, lax.axis_size(PLANE), float(LAT) ** (-1.5)), PLANE)
    own = (mode_id * mode_dev).reshape(1, 1).astype(jnp.int32)
    return exchange_rows(spins, pair_combs, pair_moms, own, triplets, perams, mode_dev)


def solution(mesh):
    fine = Mesh(mesh.devices.reshape(2, 4, 2, 8, 2), MODE + SITE)
    placed = (P(None, MODE, None, SITE), P(), P(), P(), P(SITE, None), P(SITE, None))
    return jax.shard_map(
        body, mesh=fine, in_specs=placed, out_specs=P(SITE, None, MODE, None), check_vma=False
    )
```

time: 107 us -> 83.2 us (0.78)
  blocking collectives: 40.3 us -> 30.7 us
  Pallas kernels: 23.1 us -> 16.3 us
  local copies, waits for them, and re-layouts: 6.66 us -> 1.51 us
    all_to_all x2, blocking collectives: 40.3 us -> 30.7 us  [swap(): return lax.all_to_all(x, axis, split_axis=0, concat_axis=0)]
    pallas_call x4, Pallas kernels: 13.2 us -> 8.06 us  [the longest x1 5.24 us: triplet_parts(): pl.pallas_call(triplet_kernel, out_shape=pltpu.VMEM((nslice * LANES // CH...]
    pallas_call x1 -> x0, local copies, waits for them, and re-layouts: 2.2 us -> none  [split_sites(): pl.pallas_call(split_kernel, out_shape=jax.ShapeDtypeStruct((peers, nslic...]
    unnamed x8 -> x7, local copies, waits for them, and re-layouts: 3.38 us -> 1.33 us
    pallas_call x1, Pallas kernels: 9.86 us -> 8.28 us  [exchange_rows(): pl.pallas_call(exchange_kernel, out_shape=jax.ShapeDtypeStruct((1, nslice...]
  transfers between devices with their start and end apart: 2 -> 2, of which waited for: 2 -> 2; matrix products, arithmetic and copies ran while one was open for 2% -> 1% of each run, Pallas kernels for 0% -> 0%
where the time goes in v2:
time: 83.2 us; the launch traced here: 82.7 us
  blocking collectives  30.7 us (37%)
  waiting for transfers between devices  18.9 us (23%)
  Pallas kernels  16.3 us (20%)
  starting transfers between devices  15.1 us (18%)
  local copies, waits for them, and re-layouts  1.51 us (2%)
    all_to_all x2, blocking collectives, swap(): return lax.all_to_all(x, axis, split_axis=0, concat_axis=0)  30.7 us
    all_to_all x2, waiting for transfers between devices, swap(): return lax.all_to_all(x, axis, split_axis=0, concat_axis=0)  18.9 us
    all_to_all x2, starting transfers between devices, swap(): return lax.all_to_all(x, axis, split_axis=0, concat_axis=0)  15.1 us
    pallas_call x1, Pallas kernels, exchange_rows(): pl.pallas_call(exchange_kernel, out_shape=jax.ShapeDtypeStruct((1, nslice...  8.28 us
    pallas_call x1, Pallas kernels, triplet_parts(): pl.pallas_call(triplet_kernel, out_shape=pltpu.VMEM((nslice * LANES // CH...  5.24 us
    pallas_call x1, Pallas kernels, split_sites(): pl.pallas_call(split_kernel, out_shape=pltpu.VMEM((peers, nslice * ncolor...  1.88 us
  transfers between devices with their start and end apart: 2, of which 2 were waited for; matrix products, arithmetic and copies ran while one was open for 1% of the time, Pallas kernels for 0%

profile of v2, /device:TPU:1, one launch (start us, length us, event | category | flops | bytes accessed | tf_op | source)
XLA Modules:
  0.0 82.7 jit_solution(10322711296884040929)
XLA Ops:
  0.0 1.9 %split_sites.1 = bf16[16,24,432]{2,1,0:T(8,128)(2,1)} custom-call(bf16[2,3,4,6912]{3,2,1,0:T(4,128)(2,1)} %bitcast.2), custom_call_target="tpu_custom_call" | custom-call | tf_op jit(solution)/shard_map/split_sites/pallas_call | solution.py:87
  1.9 8.4 %all-to-all-start = ((bf16[16,24,432]{2,1,0:T(8,128)(2,1)}), bf16[16,24,432]{2,1,0:T(8,128)(2,1)S(1)}, u32[]{:S(2)}, u32[]{:S(2)}) async-start(bf16[16,24,432]{2,1,0:T(8,128)(2,1)} %split_sites.1), calls=%async_computation | async-start | bytes 786432 | tf_op jit(solution)/shard_map/all_to_all | solution.py:271
  10.3 0.0 copy-start.1
  10.4 0.6 copy-done.1
  11.0 0.2 slice_reduce_fusion.2
  11.2 0.2 sine_add_fusion.phase_ref
  11.4 8.7 %all-to-all-done.x_ref = bf16[16,24,432]{2,1,0:T(8,128)(2,1)S(1)} async-done(((bf16[16,24,432]{2,1,0:T(8,128)(2,1)}), bf16[16,24,432]{2,1,0:T(8,128)(2,1)S(1)}, u32[]{:S(2)}, u32[]{:S(2)}) %all-to-all-start) | async-done | bytes 331808 | tf_op jit(solution)/shard_map/all_to_all | solution.py:271
  20.1 5.2 %triplet_parts.1 = bf16[32,16,512]{2,1,0:T(8,128)(2,1)S(1)} custom-call(bf16[16,24,432]{2,1,0:T(8,128)(2,1)S(1)} %all-to-all-done.x_ref, f32[2,512]{1,0:T(2,128)S(1)} %sine_add_fusion.phase_ref), custom_call_target="tpu_custom_call" | custom-call | tf_op jit(solution)/shard_map/triplet_parts/pallas_call | solution.py:147
  25.3 14.7 %all_to_all.20.x_ref = bf16[32,16,512]{2,1,0:T(8,128)(2,1)S(1)} all-to-all(bf16[32,16,512]{2,1,0:T(8,128)(2,1)S(1)} %triplet_parts.1), channel_id=1, replica_groups=mesh['x_hi'=2,'y'=4,'core'=2,'z'=8,'x_lo'=2] {'x_hi','y','core','x_lo'}, dimensions={0} | all-to-all | bytes 1048576 | tf_op jit(solution)/shard_map/all_to_all | solution.py:271
  40.1 0.1 sum_and_repeat.2
  40.2 15.9 %all_to_all.21.x_ref = bf16[8,16,512]{2,1,0:T(8,128)(2,1)S(1)} all-to-all(bf16[8,16,512]{2,1,0:T(8,128)(2,1)S(1)} %sum_and_repeat.2), channel_id=1, replica_groups=mesh['x_hi'=2,'y'=4,'core'=2,'z'=8,'x_lo'=2] {'z'}, dimensions={0} | all-to-all | bytes 262144 | tf_op jit(solution)/shard_map/all_to_all | solution.py:271
  56.1 0.9 %sum_and_repeat.3 = bf16[32,16,512]{2,1,0:T(8,128)(2,1)} custom-call(bf16[8,16,512]{2,1,0:T(8,128)(2,1)S(1)} %all_to_all.21.x_ref), custom_call_target="tpu_custom_call" | custom-call | tf_op jit(solution)/shard_map/sum_and_repeat/pallas_call | solution.py:175
  56.9 0.0 copy-start.2
  56.9 0.0 copy-start
  56.9 6.7 %all-to-all-start.3 = ((bf16[32,16,512]{2,1,0:T(8,128)(2,1)}), bf16[32,16,512]{2,1,0:T(8,128)(2,1)S(1)}, u32[]{:S(2)}, u32[]{:S(2)}) async-start(bf16[32,16,512]{2,1,0:T(8,128)(2,1)} %sum_and_repeat.3), calls=%async_computation.3 | async-start | bytes 1048576 | tf_op jit(solution)/shard_map/all_to_all | solution.py:271
  63.6 0.0 copy-done.2
  63.7 0.7 copy.8.spins_ref
  64.3 10.1 %all-to-all-done.3.tri_ref = bf16[32,16,512]{2,1,0:T(8,128)(2,1)S(1)} async-done(((bf16[32,16,512]{2,1,0:T(8,128)(2,1)}), bf16[32,16,512]{2,1,0:T(8,128)(2,1)S(1)}, u32[]{:S(2)}, u32[]{:S(2)}) %all-to-all-start.3) | async-done | bytes 524320 | tf_op jit(solution)/shard_map/all_to_all | solution.py:271
  74.5 0.0 copy-done
  74.5 8.3 %exchange_rows.1 = f32[1,2,4,64]{3,2,1,0:T(4,128)} custom-call(s32[16,3]{1,0:T(8,128)} %copy.8.spins_ref, s32[1,2]{1,0:T(1,128)} %combs_ref.1, s32[1,2]{1,0:T(1,128)} %moms_ref.1, s32[1,1]{1,0:T(1,128)} %bitcast.own_ref, bf16[32,16,512]{2,1,0:T(8,128)(2,1)S(1)} %all-to-all-done.3.tri_ref, bf16[2,16,64,64]{3,2,1,0:T(8,128)(2,1)S(1)} %copy-done, ...), custom_call_target="tpu_custom_call" | custom-call | tf_op jit(solution)/shard_map/exchange_rows/pallas_call | solution.py:247
  (2 shorter events, 0.0 us)
Async XLA Ops:
  1.9 18.2 %all-to-all-start = ((bf16[16,24,432]{2,1,0:T(8,128)(2,1)}), bf16[16,24,432]{2,1,0:T(8,128)(2,1)S(1)}, u32[]{:S(2)}, u32[]{:S(2)}) async-start(bf16[16,24,432]{2,1,0:T(8,128)(2,1)} %split_sites.1), calls=%async_computation | async-start | bytes 786432 | tf_op jit(solution)/shard_map/all_to_all | solution.py:271
  10.3 0.7 copy-start.1
  56.9 6.7 %copy-start.2 = (s32[16,3]{0,1:T(4,128)S(1)}, s32[16,3]{0,1:T(4,128)}, u32[]{:S(2)}) copy-start(s32[16,3]{0,1:T(4,128)} %param.10) | copy-start | bytes 580
  56.9 17.5 %copy-start = (bf16[2,16,64,64]{3,2,1,0:T(8,128)(2,1)S(1)}, bf16[2,16,64,64]{3,2,1,0:T(8,128)(2,1)}, u32[]{:S(2)}) copy-start(bf16[2,16,64,64]{3,2,1,0:T(8,128)(2,1)} %per_ref.1) | copy-start | bytes 786436
  56.9 17.5 %all-to-all-start.3 = ((bf16[32,16,512]{2,1,0:T(8,128)(2,1)}), bf16[32,16,512]{2,1,0:T(8,128)(2,1)S(1)}, u32[]{:S(2)}, u32[]{:S(2)}) async-start(bf16[32,16,512]{2,1,0:T(8,128)(2,1)} %sum_and_repeat.3), calls=%async_computation.3 | async-start | bytes 1048576 | tf_op jit(solution)/shard_map/all_to_all | solution.py:271
